TPU v7x, 32 devices: a whole 2x2x4 slice. The times are simulated.
32 devices in a mesh: depth: 2 (over core), row: 4 (over y, x), col: 4 (over z).
Axes of the slice: x: 2, y: 2, z: 4, core: 2. Of those that a mesh axis runs over, the one named last changes fastest.
Arguments:
- tile_left: bfloat16 [16, 16, 64, 1024], P('row', 'col'), may hold values from -6 to 6
- tile_right: bfloat16 [16, 16, 64, 1024], P('row', 'col'), may hold values from -6 to 6
- row_left: bfloat16 [16, 8, 64, 1024], P('row', 'depth', None, 'col'), may hold values from -6 to 6
- row_right: bfloat16 [16, 8, 64, 1024], P('row', 'depth', None, 'col'), may hold values from -0.1875 to 0.1875
- col_left: bfloat16 [16, 8, 64, 1024], P('col', 'depth', None, 'row'), may hold values from -6 to 6
- col_right: bfloat16 [16, 8, 64, 1024], P('col', 'depth', None, 'row'), may hold values from -0.1875 to 0.1875
- row_mask: int32 [16, 8], P('row', 'depth'), may hold values 0 or 1
- col_mask: int32 [16, 8], P('col', 'depth'), may hold values 0 or 1
- sketch: bfloat16 [64, 1024], replicated, may hold values from -1 to 1
Outputs:
- new_left: float32 [16, 16, 64, 1024], P('row', 'col', 'depth')
- new_right: float32 [16, 16, 64, 1024], P('row', 'col', 'depth')
All inputs are finite; a program needn't handle non-finite values. No bound on the sum of `row_mask` or of `col_mask` on one device may be relied on, other than what follows from the above.
Results may differ from a plain program's by a relative error of at most 0.0003.
Values may be sent and summed in bfloat16 or wider, within the bound.
No kernel may reach another device: no remote copies, remote signals or barrier semaphores. Data moves between devices by JAX's collectives and lax.ppermute only.
A program may use at most 64 MiB of HBM per device.

v0:
```python
import math
import jax
import jax.numpy as jnp
from jax import lax
from jax.sharding import PartitionSpec as P

NB = 1024
K = 64
exact_mode = lax.Precision.HIGHEST


def orthonormalize(sketched):
    for repeat in range(2):
        gram_mat = jnp.einsum("ijtn,ijsn->ijts", sketched, sketched, precision=exact_mode)
        factor = jnp.linalg.cholesky(gram_mat)
        sketched = jax.scipy.linalg.solve_triangular(factor, sketched, lower=True)
    return sketched


def on_device(
    tile_left, tile_right, row_left, row_right, col_left, col_right, row_mask, col_mask, sketch
):
    row_full_left, row_full_right = (
        lax.all_gather(row_left, "col", axis=3, tiled=True),
        lax.all_gather(row_right, "col", axis=3, tiled=True),
    )
    col_full_left, col_full_right = (
        lax.all_gather(col_left, "row", axis=3, tiled=True),
        lax.all_gather(col_right, "row", axis=3, tiled=True),
    )
    weight_table = (
        row_mask.astype(jnp.float32)[:, None, :] * col_mask.astype(jnp.float32)[None, :, :]
    )
    coupling = jnp.einsum(
        "ikrn,jksn->ijkrs", row_full_right, col_full_right, preferred_element_type=jnp.float32
    )
    coupling = coupling * weight_table[:, :, :, None, None]
    col_sketch = jnp.einsum(
        "jksn,tn->jkst", col_full_left, sketch, preferred_element_type=jnp.float32
    )
    mixing = jnp.einsum("ijkrs,jkst->ijkrt", coupling, col_sketch, precision=exact_mode)
    partial_sketch = -jnp.einsum(
        "ijkrt,ikrn->ijtn",
        mixing,
        row_full_left,
        precision=exact_mode,
        preferred_element_type=jnp.float32,
    )
    sketch_right = jnp.einsum(
        "ijrn,tn->ijrt", tile_right, sketch, preferred_element_type=jnp.float32
    )
    summed = lax.psum(partial_sketch, "depth")
    sketched = summed + jnp.einsum(
        "ijrt,ijrn->ijtn",
        sketch_right,
        tile_left,
        precision=exact_mode,
        preferred_element_type=jnp.float32,
    )
    basis = orthonormalize(sketched)
    rank_rows = K // lax.axis_size("depth")
    rank_offset = lax.axis_index("depth") * rank_rows
    basis_mine = lax.dynamic_slice_in_dim(basis, rank_offset, rank_rows, 2)
    basis_row = jnp.einsum(
        "ijtn,ikrn->ijktr",
        basis,
        row_full_left,
        precision=exact_mode,
        preferred_element_type=jnp.float32,
    )
    projected = jnp.einsum("ijktr,ijkrs->ijkts", basis_row, coupling, precision=exact_mode)
    right_part = -jnp.einsum(
        "ijkts,jksn->ijtn",
        projected,
        col_full_left,
        precision=exact_mode,
        preferred_element_type=jnp.float32,
    )
    right_share = lax.psum_scatter(right_part, "depth", scatter_dimension=2, tiled=True)
    own_part = jnp.einsum(
        "ijtn,ijrn->ijtr",
        basis_mine,
        tile_left,
        precision=exact_mode,
        preferred_element_type=jnp.float32,
    )
    right_share = right_share + jnp.einsum(
        "ijtr,ijrn->ijtn",
        own_part,
        tile_right,
        precision=exact_mode,
        preferred_element_type=jnp.float32,
    )
    return (basis_mine * math.sqrt(NB), right_share / math.sqrt(NB))


def solution(mesh):
    in_specs = (
        P("row", "col", None, None),
        P("row", "col", None, None),
        P("row", "depth", None, "col"),
        P("row", "depth", None, "col"),
        P("col", "depth", None, "row"),
        P("col", "depth", None, "row"),
        P("row", "depth"),
        P("col", "depth"),
        P(),
    )
    out_specs = (P("row", "col", "depth", None), P("row", "col", "depth", None))
    return jax.shard_map(
        on_device, mesh=mesh, in_specs=in_specs, out_specs=out_specs, check_vma=False
    )
```

profile of v0, /device:TPU:0, one launch (start us, length us, event | category | flops | bytes accessed | tf_op | source)
XLA Modules:
  0.0 626.7 jit_solution(12347719536717495241)
XLA Ops:
  7.2 0.0 copy-start
  7.2 0.0 all-gather.5.cloned.1.call-start
  7.3 0.7 all-gather.5.cloned.1.call-update
  8.0 0.0 all-gather.7.cloned.1.call-start
  8.0 1.9 copy.21
  9.9 0.0 all-gather.7.cloned.1.call-update
  9.9 0.0 all-gather.9.cloned.1.call-start
  10.0 0.8 copy.22
  10.8 0.0 all-gather.9.cloned.1.call-update
  10.8 0.0 all-gather.11.cloned.1.call-start
  10.9 0.5 all-gather.11.cloned.1.call-update
  11.4 0.0 all-reduce.2.cloned.1.call-start
  11.5 0.1 copy.23
  11.6 0.1 copy.24
  11.7 0.1 broadcast_multiply_fusion
  11.8 35.9 %all-gather.5.cloned.1.call-done = bf16[4,4,64,1024]{3,2,1,0:T(8,128)(2,1)} async-done(((bf16[4,4,64,256]{3,2,1,0:T(8,128)(2,1)}), bf16[4,4,64,1024]{3,2,1,0:T(8,128)(2,1)}) %all-gather.5.cloned.1.call-update) | async-done | bytes 2097168 | tf_op jit(solution)/shard_map/all_gather | solution.py:28
  47.7 0.0 copy-done.10
  47.7 2.3 convolution_bitcast_fusion
  49.9 35.2 %all-gather.7.cloned.1.call-done = bf16[4,4,64,1024]{3,2,0,1:T(8,128)(2,1)} async-done(((bf16[4,4,64,256]{3,2,0,1:T(8,128)(2,1)}), bf16[4,4,64,1024]{3,2,0,1:T(8,128)(2,1)}) %all-gather.7.cloned.1.call-update) | async-done | bytes 2097168 | tf_op jit(solution)/shard_map/all_gather | solution.py:29
  85.1 48.4 %all-gather.9.cloned.1.call-done = bf16[4,4,64,1024]{3,2,0,1:T(8,128)(2,1)} async-done(((bf16[4,4,64,256]{3,2,0,1:T(8,128)(2,1)}), bf16[4,4,64,1024]{3,2,0,1:T(8,128)(2,1)}) %all-gather.9.cloned.1.call-update) | async-done | bytes 2097168 | tf_op jit(solution)/shard_map/all_gather | solution.py:25
  133.6 3.5 bitcast_multiply_fusion
  137.1 0.0 copy-start.6
  137.1 1.3 copy-done.6
  138.4 3.3 fusion.15
  141.7 37.8 %all-gather.11.cloned.1.call-done = bf16[4,4,64,1024]{3,2,1,0:T(8,128)(2,1)} async-done(((bf16[4,4,64,256]{3,2,1,0:T(8,128)(2,1)}), bf16[4,4,64,1024]{3,2,1,0:T(8,128)(2,1)}) %all-gather.11.cloned.1.call-update) | async-done | bytes 2097168 | tf_op jit(solution)/shard_map/all_gather | solution.py:24
  179.5 6.2 bitcast_negate_fusion.1
  185.6 0.0 all-reduce.2.cloned.1.call-update
  185.6 0.3 reduce-scatter.2.cloned.1.call-start
  186.0 2.7 fusion.32
  188.7 23.4 %all-reduce.2.cloned.1.call-done = f32[4,4,64,1024]{3,2,1,0:T(8,128)} async-done(((f32[4,4,64,1024]{3,2,1,0:T(8,128)}), f32[4,4,64,1024]{3,2,1,0:T(8,128)}) %all-reduce.2.cloned.1.call-update) | async-done | bytes 4194320 | tf_op jit(solution)/shard_map/psum | solution.py:52
  212.1 4.1 convolution_add_fusion
  216.2 1.9 copy-done.2
  218.2 4.0 fusion.36
  222.2 0.2 copy.25
  222.4 0.9 fusion.30
  223.3 95.0 %custom-call.8 = f32[4,4,64,64]{3,2,1,0:T(8,128)S(1)} custom-call(f32[4,4,64,64]{3,2,1,0:T(8,128)} %fusion.30), custom_call_target="Cholesky" | custom-call | tf_op jit(solution)/shard_map/jit(cholesky)/cholesky | solution.py:15
  318.3 0.1 select_reduce_fusion.1
  318.3 0.1 compare_reduce_fusion.1
  318.5 0.1 select_bitcast_fusion.1
  318.6 78.6 %custom-call.9 = f32[4,4,1,64,64]{3,4,2,1,0:T(8,128)S(1)} custom-call(f32[4,4,1,64,64]{4,3,2,1,0:T(8,128)S(1)} %select_bitcast_fusion.1), custom_call_target="InvertDiagBlocksLowerTriangular" | custom-call | tf_op jit(solution)/shard_map/jit(_solve_triangular)/vmap(vmap())/triangular_solve | solution.py:16
  397.3 5.5 fusion.28
  402.8 1.9 copy-done.1
  404.7 4.0 fusion.37
  408.8 0.2 copy.27
  409.0 0.9 fusion.27
  409.8 94.5 %custom-call.10 = f32[4,4,64,64]{3,2,1,0:T(8,128)S(1)} custom-call(f32[4,4,64,64]{3,2,1,0:T(8,128)} %fusion.27), custom_call_target="Cholesky" | custom-call | tf_op jit(solution)/shard_map/jit(cholesky)/cholesky | solution.py:15
  504.3 0.1 select_reduce_fusion
  504.4 0.1 compare_reduce_fusion
  504.6 0.1 select_bitcast_fusion
  504.7 78.6 %custom-call.11 = f32[4,4,1,64,64]{3,4,2,1,0:T(8,128)S(1)} custom-call(f32[4,4,1,64,64]{4,3,2,1,0:T(8,128)S(1)} %select_bitcast_fusion), custom_call_target="InvertDiagBlocksLowerTriangular" | custom-call | tf_op jit(solution)/shard_map/jit(_solve_triangular)/vmap(vmap())/triangular_solve | solution.py:16
  583.3 0.0 copy-start.5
  583.4 5.8 fusion.25
  589.2 3.5 fusion
  592.6 0.0 copy-start.7
  592.7 1.4 copy.61
  594.1 0.2 copy-done.7
  594.2 3.5 fusion.12
  597.8 3.7 fusion.2
  601.4 0.0 reduce-scatter.2.cloned.1.call-update
  601.5 3.4 dynamic-slice_multiply_fusion
  604.9 1.8 fusion.17
  606.7 8.1 %reduce-scatter.2.cloned.1.call-done = f32[4,4,32,1024]{3,2,0,1:T(8,128)} async-done(((f32[4,4,64,1024]{3,2,0,1:T(8,128)}), f32[4,4,32,1024]{3,2,0,1:T(8,128)}) %reduce-scatter.2.cloned.1.call-update) | async-done | bytes 2097168 | tf_op jit(solution)/shard_map/reduce_scatter | solution.py:79
  614.8 3.3 add_multiply_fusion
  618.2 1.5 copy.30
  (21 shorter events, 0.1 us)
Async XLA Ops:
  7.2 204.9 %copy-start = (bf16[4,4,64,1024]{3,2,1,0:T(8,128)(2,1)S(1)}, bf16[4,4,64,1024]{3,2,1,0:T(8,128)(2,1)}, u32[]{:S(2)}) copy-start(bf16[4,4,64,1024]{3,2,1,0:T(8,128)(2,1)} %param.12) | copy-start | bytes 6291460
  7.2 2.8 copy-start.9
  7.2 4.3 copy-start.11
  7.2 4.4 copy-start.12
  7.2 40.4 %copy-start.10 = (bf16[64,1024]{1,0:T(8,128)(2,1)S(1)}, bf16[64,1024]{1,0:T(8,128)(2,1)}, u32[]{:S(2)}) copy-start(bf16[64,1024]{1,0:T(8,128)(2,1)} %param.20) | copy-start | bytes 393220
  7.2 40.4 %all-gather.5.cloned.1.call-start = ((), (), s32[]{:S(2)}) async-start(), calls=%async_computation.1 | async-start | bytes 2621440 | tf_op jit(solution)/shard_map/all_gather | solution.py:28
  8.0 77.2 %all-gather.7.cloned.1.call-start = ((), (), s32[]{:S(2)}) async-start(), calls=%async_computation.2 | async-start | bytes 2621440 | tf_op jit(solution)/shard_map/all_gather | solution.py:29
  9.9 123.6 %all-gather.9.cloned.1.call-start = ((), (), s32[]{:S(2)}) async-start(), calls=%async_computation.3 | async-start | bytes 2621440 | tf_op jit(solution)/shard_map/all_gather | solution.py:25
  10.8 168.6 %all-gather.11.cloned.1.call-start = ((), (), s32[]{:S(2)}) async-start(), calls=%async_computation.4 | async-start | bytes 2621440 | tf_op jit(solution)/shard_map/all_gather | solution.py:24
  11.4 200.7 %all-reduce.2.cloned.1.call-start = ((), (), s32[]{:S(2)}) async-start(), calls=%async_computation.5 | async-start | bytes 8388608 | tf_op jit(solution)/shard_map/psum | solution.py:52
  137.1 1.3 copy-start.6
  185.6 429.2 %reduce-scatter.2.cloned.1.call-start = ((), (), s32[]{:S(2)}) async-start(), calls=%async_computation.6 | async-start | bytes 6291456 | tf_op jit(solution)/shard_map/reduce_scatter | solution.py:79
  216.2 1.9 copy-start.2
  402.8 1.9 copy-start.1
  583.3 5.8 copy-start.5
  589.2 3.5 copy-start.3
  592.6 1.6 copy-start.7
  594.2 3.5 copy-start.8
  601.5 3.4 copy-start.4
Sparse Core Ops, SparseCore 0:
  9.9 37.7 all-gather.4
  50.1 35.0 all-gather.6
  87.3 46.2 all-gather.8
  135.0 44.4 all-gather.10
  185.8 26.2 all-reduce.1
  601.6 13.2 reduce-scatter.1
where the time goes:
time: 632 us; the launch traced here: 627 us
  other arithmetic  353 us (56%)
  waiting for transfers between devices  190 us (30%)
  matrix products  57.2 us (9%)
  between operations  14.6 us (2%)
  local copies, waits for them, and re-layouts  11.6 us (2%)
    another operation x7, other arithmetic, orthonormalize(): factor = jnp.linalg.cholesky(gram_mat)  190 us
    another operation x5, other arithmetic, orthonormalize(): sketched = jax.scipy.linalg.solve_triangular(factor, sketched, lower=True)  158 us
    all_gather x1, waiting for transfers between devices, on_device(): lax.all_gather(row_right, 'col', axis=3, tiled=True)  48.4 us
    all_gather x1, waiting for transfers between devices, on_device(): lax.all_gather(row_left, 'col', axis=3, tiled=True)  37.8 us
    all_gather x1, waiting for transfers between devices, on_device(): lax.all_gather(col_left, 'row', axis=3, tiled=True)  35.9 us
    all_gather x1, waiting for transfers between devices, on_device(): lax.all_gather(col_right, 'row', axis=3, tiled=True)  35.2 us
    psum x1, waiting for transfers between devices, on_device(): summed = lax.psum(partial_sketch, 'depth')  23.4 us
  transfers between devices with their start and end apart: 6, of which 6 were waited for; matrix products, arithmetic and copies ran while one was open for 3% of the time, Pallas kernels for 0%

commit v1 on v0

--- a/solution.py
+++ b/solution.py
@@ -25,7 +25,9 @@
         lax.all_gather(row_right, "col", axis=3, tiled=True),
     )
     col_full_left, col_full_right = (
-        lax.all_gather(col_left, "row", axis=3, tiled=True),
+        jnp.concatenate(
+            lax.all_to_all(jnp.stack([col_left] * lax.axis_size("row")), "row", 0, 0), axis=3
+        ),
         lax.all_gather(col_right, "row", axis=3, tiled=True),
     )
     weight_table = (

time: 632 us -> 610 us (0.965)
  waiting for transfers between devices: 190 us -> 150 us
  local copies, waits for them, and re-layouts: 11.6 us -> 24.7 us
    all_gather x1 -> x0, waiting for transfers between devices: 35.9 us -> none  [on_device(): lax.all_gather(col_left, 'row', axis=3, tiled=True)]
    all_to_all x0 -> x1, waiting for transfers between devices: none -> 31 us  [on_device(): lax.all_to_all(jnp.stack([col_left] * lax.axis_size('row')), 'row', 0, 0)]
    all_gather x1, waiting for transfers between devices: 35.2 us -> 10.3 us  [on_device(): lax.all_gather(col_right, 'row', axis=3, tiled=True)]
    reshape x0 -> x3, local copies, waits for them, and re-layouts: none -> 11.9 us  [on_device(): jnp.concatenate(lax.all_to_all(jnp.stack([col_left] * lax.axis_size('row'...]
    psum x1, waiting for transfers between devices: 23.4 us -> 13.7 us  [on_device(): summed = lax.psum(partial_sketch, 'depth')]
  transfers between devices with their start and end apart: 6 -> 6, of which waited for: 6 -> 6; matrix products, arithmetic and copies ran while one was open for 3% -> 5% of each run, Pallas kernels for 0% -> 0%
where the time goes in v1:
time: 610 us; the launch traced here: 603 us
  other arithmetic  352 us (58%)
  waiting for transfers between devices  150 us (25%)
  matrix products  55.8 us (9%)
  local copies, waits for them, and re-layouts  24.7 us (4%)
  between operations  14.3 us (2%)
    another operation x7, other arithmetic, orthonormalize(): factor = jnp.linalg.cholesky(gram_mat)  189 us
    another operation x5, other arithmetic, orthonormalize(): sketched = jax.scipy.linalg.solve_triangular(factor, sketched, lower=True)  158 us
    all_gather x1, waiting for transfers between devices, on_device(): lax.all_gather(row_right, 'col', axis=3, tiled=True)  48.4 us
    all_gather x1, waiting for transfers between devices, on_device(): lax.all_gather(row_left, 'col', axis=3, tiled=True)  38.1 us
    all_to_all x1, waiting for transfers between devices, on_device(): lax.all_to_all(jnp.stack([col_left] * lax.axis_size('row')), 'row', 0, 0)  31 us
    psum x1, waiting for transfers between devices, on_device(): summed = lax.psum(partial_sketch, 'depth')  13.7 us
  transfers between devices with their start and end apart: 6, of which 6 were waited for; matrix products, arithmetic and copies ran while one was open for 5% of the time, Pallas kernels for 0%

profile of v1, /device:TPU:0, one launch (start us, length us, event | category | flops | bytes accessed | tf_op | source)
XLA Modules:
  0.0 603.0 jit_solution(915645128005304492)
XLA Ops:
  7.2 0.0 copy-start
  7.2 0.0 all-gather.4.cloned.1.call-start
  7.2 2.1 copy.33
  9.3 0.0 all-gather.4.cloned.1.call-update
  9.3 0.0 all-gather.6.cloned.1.call-start
  9.4 1.9 copy.34
  11.3 0.0 all-gather.6.cloned.1.call-update
  11.3 0.0 all-gather.8.cloned.1.call-start
  11.3 0.7 all-gather.8.cloned.1.call-update
  12.0 0.0 copy-done.9
  12.0 1.6 stack.2
  13.6 5.3 all-to-all-start
  19.0 0.1 copy.35
  19.1 0.1 copy.36
  19.2 0.1 broadcast_multiply_fusion
  19.2 31.0 %all-to-all-done = bf16[4,4,4,64,256]{4,3,2,1,0:T(8,128)(2,1)} async-done(((bf16[4,4,4,64,256]{4,3,2,1,0:T(8,128)(2,1)}), bf16[4,4,4,64,256]{4,3,2,1,0:T(8,128)(2,1)}, u32[]{:S(2)}, u32[]{:S(2)}) %all-to-all-start) | async-done | bytes 2097184 | tf_op jit(solution)/shard_map/all_to_all | solution.py:29
  50.3 2.0 copy.67
  52.3 1.1 convolution_bitcast_fusion
  53.4 10.3 %all-gather.4.cloned.1.call-done = bf16[4,4,64,1024]{3,2,0,1:T(8,128)(2,1)} async-done(((bf16[4,4,64,256]{3,2,0,1:T(8,128)(2,1)}), bf16[4,4,64,1024]{3,2,0,1:T(8,128)(2,1)}) %all-gather.4.cloned.1.call-update) | async-done | bytes 2097168 | tf_op jit(solution)/shard_map/all_gather | solution.py:31
  63.7 48.4 %all-gather.6.cloned.1.call-done = bf16[4,4,64,1024]{3,2,0,1:T(8,128)(2,1)} async-done(((bf16[4,4,64,256]{3,2,0,1:T(8,128)(2,1)}), bf16[4,4,64,1024]{3,2,0,1:T(8,128)(2,1)}) %all-gather.6.cloned.1.call-update) | async-done | bytes 2097168 | tf_op jit(solution)/shard_map/all_gather | solution.py:25
  112.1 3.5 bitcast_multiply_fusion
  115.6 0.0 copy-start.6
  115.6 1.3 copy-done.6
  116.9 3.1 fusion.12
  120.1 38.1 %all-gather.8.cloned.1.call-done = bf16[4,4,64,1024]{3,2,1,0:T(8,128)(2,1)} async-done(((bf16[4,4,64,256]{3,2,1,0:T(8,128)(2,1)}), bf16[4,4,64,1024]{3,2,1,0:T(8,128)(2,1)}) %all-gather.8.cloned.1.call-update) | async-done | bytes 2097168 | tf_op jit(solution)/shard_map/all_gather | solution.py:24
  158.2 6.2 %bitcast_negate_fusion.1 = f32[4,4,64,1024]{3,2,1,0:T(8,128)} fusion(bf16[4,4,64,1024]{3,2,1,0:T(8,128)(2,1)} %all-gather.8.cloned.1.call-done, f32[4,4,64,4,64]{4,2,1,0,3:T(8,128)} %fusion.12), kind=kOutput, calls=%fused_computation.4 | convolution fusion | flops 3222274048 | bytes 7340032 | tf_op jit(solution)/shard_map/ijkrt,ikrn->ijtn/dot_general | solution.py:44
  164.3 0.0 all-reduce.2.cloned.1.call-update
  164.4 0.0 reduce-scatter.2.cloned.1.call-start
  164.4 2.7 fusion.37
  167.1 5.0 copy.32
  172.1 4.9 reshape.33
  177.1 13.7 %all-reduce.2.cloned.1.call-done = f32[4,4,64,1024]{3,2,1,0:T(8,128)} async-done(((f32[4,4,64,1024]{3,2,1,0:T(8,128)}), f32[4,4,64,1024]{3,2,1,0:T(8,128)}) %all-reduce.2.cloned.1.call-update) | async-done | bytes 4194320 | tf_op jit(solution)/shard_map/psum | solution.py:54
  190.8 4.1 convolution_add_fusion
  194.9 1.9 copy-done.2
  196.9 4.0 fusion.41
  200.9 0.2 copy.40
  201.1 0.9 fusion.35
  202.0 94.5 %custom-call.8 = f32[4,4,64,64]{3,2,1,0:T(8,128)S(1)} custom-call(f32[4,4,64,64]{3,2,1,0:T(8,128)} %fusion.35), custom_call_target="Cholesky" | custom-call | tf_op jit(solution)/shard_map/jit(cholesky)/cholesky | solution.py:15
  296.5 0.1 select_reduce_fusion.1
  296.5 0.1 compare_reduce_fusion.1
  296.7 0.1 select_bitcast_fusion.1
  296.8 78.6 %custom-call.9 = f32[4,4,1,64,64]{3,4,2,1,0:T(8,128)S(1)} custom-call(f32[4,4,1,64,64]{4,3,2,1,0:T(8,128)S(1)} %select_bitcast_fusion.1), custom_call_target="InvertDiagBlocksLowerTriangular" | custom-call | tf_op jit(solution)/shard_map/jit(_solve_triangular)/vmap(vmap())/triangular_solve | solution.py:16
  375.5 5.7 fusion.33
  381.2 1.9 copy-done.1
  383.1 4.0 fusion.42
  387.1 0.2 copy.42
  387.4 0.9 fusion.32
  388.2 94.5 %custom-call.10 = f32[4,4,64,64]{3,2,1,0:T(8,128)S(1)} custom-call(f32[4,4,64,64]{3,2,1,0:T(8,128)} %fusion.32), custom_call_target="Cholesky" | custom-call | tf_op jit(solution)/shard_map/jit(cholesky)/cholesky | solution.py:15
  482.7 0.1 select_reduce_fusion
  482.8 0.1 compare_reduce_fusion
  482.9 0.1 select_bitcast_fusion
  483.1 78.6 %custom-call.11 = f32[4,4,1,64,64]{3,4,2,1,0:T(8,128)S(1)} custom-call(f32[4,4,1,64,64]{4,3,2,1,0:T(8,128)S(1)} %select_bitcast_fusion), custom_call_target="InvertDiagBlocksLowerTriangular" | custom-call | tf_op jit(solution)/shard_map/jit(_solve_triangular)/vmap(vmap())/triangular_solve | solution.py:16
  561.7 0.0 copy-start.5
  561.7 5.8 fusion.30
  567.6 0.0 copy-start.7
  567.6 3.5 fusion.23
  571.1 3.5 fusion.7
  574.6 3.5 fusion.2
  578.1 0.0 reduce-scatter.2.cloned.1.call-update
  578.1 3.4 dynamic-slice_multiply_fusion
  581.5 1.8 fusion.17
  583.3 8.1 %reduce-scatter.2.cloned.1.call-done = f32[4,4,32,1024]{3,2,0,1:T(8,128)} async-done(((f32[4,4,64,1024]{3,2,0,1:T(8,128)}), f32[4,4,32,1024]{3,2,0,1:T(8,128)}) %reduce-scatter.2.cloned.1.call-update) | async-done | bytes 2097168 | tf_op jit(solution)/shard_map/reduce_scatter | solution.py:81
  591.5 3.3 add_multiply_fusion
  594.8 1.5 copy.47
  (23 shorter events, 0.1 us)
Async XLA Ops:
  7.2 183.6 %copy-start = (bf16[4,4,64,1024]{3,2,1,0:T(8,128)(2,1)S(1)}, bf16[4,4,64,1024]{3,2,1,0:T(8,128)(2,1)}, u32[]{:S(2)}) copy-start(bf16[4,4,64,1024]{3,2,1,0:T(8,128)(2,1)} %param.12) | copy-start | bytes 6291460
  7.2 4.8 copy-start.9
  7.2 56.5 %all-gather.4.cloned.1.call-start = ((), (), s32[]{:S(2)}) async-start(), calls=%async_computation.2 | async-start | bytes 2621440 | tf_op jit(solution)/shard_map/all_gather | solution.py:31
  9.3 102.8 %all-gather.6.cloned.1.call-start = ((), (), s32[]{:S(2)}) async-start(), calls=%async_computation.3 | async-start | bytes 2621440 | tf_op jit(solution)/shard_map/all_gather | solution.py:25
  11.3 146.9 %all-gather.8.cloned.1.call-start = ((), (), s32[]{:S(2)}) async-start(), calls=%async_computation.4 | async-start | bytes 2621440 | tf_op jit(solution)/shard_map/all_gather | solution.py:24
  13.6 5.3 copy-start.11
  13.6 5.4 copy-start.12
  13.6 36.6 %all-to-all-start = ((bf16[4,4,4,64,256]{4,3,2,1,0:T(8,128)(2,1)}), bf16[4,4,4,64,256]{4,3,2,1,0:T(8,128)(2,1)}, u32[]{:S(2)}, u32[]{:S(2)}) async-start(bf16[4,4,4,64,256]{4,3,2,1,0:T(8,128)(2,1)} %stack.2), calls=%async_computation | async-start | bytes 4194304 | tf_op jit(solution)/shard_map/all_to_all | solution.py:29
  19.0 171.8 %all-reduce.2.cloned.1.call-start = ((), (), s32[]{:S(2)}) async-start(), calls=%async_computation.5 | async-start | bytes 8388608 | tf_op jit(solution)/shard_map/psum | solution.py:54
  50.3 2.0 copy-start.10
  115.6 1.3 copy-start.6
  164.4 427.1 %reduce-scatter.2.cloned.1.call-start = ((), (), s32[]{:S(2)}) async-start(), calls=%async_computation.6 | async-start | bytes 6291456 | tf_op jit(solution)/shard_map/reduce_scatter | solution.py:81
  194.9 2.0 copy-start.2
  381.2 2.0 copy-start.1
  561.7 5.9 copy-start.5
  567.6 3.5 copy-start.3
  567.6 3.5 copy-start.7
  571.1 3.5 copy-start.8
  578.1 3.4 copy-start.4
Sparse Core Ops, SparseCore 0:
  9.8 53.8 all-gather.3
  65.8 46.2 all-gather.5
  113.7 44.4 all-gather.7
  164.5 26.2 all-reduce.1
  578.2 13.2 reduce-scatter.1
